TPU v7x, 32 devices: a whole 2x2x4 slice. The times are simulated.
32 devices in a mesh: rep: 8 (over y, x, core), shard: 4 (over z).
Axes of the slice: x: 2, y: 2, z: 4, core: 2. Of those that a mesh axis runs over, the one named last changes fastest.
Arguments:
- block_in: float32 [4096, 1024], P(('rep', 'shard')), may hold values from -6 to 6
- cotangent: float32 [4096, 1024], P(('rep', 'shard')), may hold values from -0.09375 to 0.09375
- segments: int32 [8, 512], P('rep'), may hold values from 0 to 3, never falling along the last dimension, each value on 1 to 224 neighbouring positions
- qkv_weight: float32 [1024, 3072], P(('rep', 'shard')), may hold values from -0.1875 to 0.1875
- out_weight: float32 [1024, 1024], P(('rep', 'shard')), may hold values from -0.75 to 0.75
- up_weight: float32 [1024, 4096], P(('rep', 'shard')), may hold values from -0.1875 to 0.1875
- down_weight: float32 [4096, 1024], P(('rep', 'shard')), may hold values from -0.09375 to 0.09375
- vectors: float32 [13, 1024], P(None, ('rep', 'shard')), may hold values from -0.9 to 1.5, as said below
- first_qkv: float32 [1024, 3072], P(('rep', 'shard')), may hold values from -1.8 to 1.8
- first_out: float32 [1024, 1024], P(('rep', 'shard')), may hold values from -1.8 to 1.8
- first_up: float32 [1024, 4096], P(('rep', 'shard')), may hold values from -1.8 to 1.8
- first_down: float32 [4096, 1024], P(('rep', 'shard')), may hold values from -1.8 to 1.8
- first_vec: float32 [13, 1024], P(None, ('rep', 'shard')), may hold values from -1.8 to 1.8
- second_qkv: float32 [1024, 3072], P(('rep', 'shard')), may hold values from 0.002 to 0.2
- second_out: float32 [1024, 1024], P(('rep', 'shard')), may hold values from 0.002 to 0.2
- second_up: float32 [1024, 4096], P(('rep', 'shard')), may hold values from 0.002 to 0.2
- second_down: float32 [4096, 1024], P(('rep', 'shard')), may hold values from 0.002 to 0.2
- second_vec: float32 [13, 1024], P(None, ('rep', 'shard')), may hold values from 0.002 to 0.2
Outputs:
- block_out: float32 [4096, 1024], P(('rep', 'shard'))
- grad_input: float32 [4096, 1024], P(('rep', 'shard'))
- grad_qkv: float32 [1024, 3072], P(('rep', 'shard'))
- grad_out: float32 [1024, 1024], P(('rep', 'shard'))
- grad_up: float32 [1024, 4096], P(('rep', 'shard'))
- grad_down: float32 [4096, 1024], P(('rep', 'shard'))
- grad_vec: float32 [13, 1024], P(None, ('rep', 'shard'))
- new_qkv: float32 [1024, 3072], P(('rep', 'shard'))
- new_out: float32 [1024, 1024], P(('rep', 'shard'))
- new_up: float32 [1024, 4096], P(('rep', 'shard'))
- new_down: float32 [4096, 1024], P(('rep', 'shard'))
- new_vec: float32 [13, 1024], P(None, ('rep', 'shard'))
- new_first_qkv: float32 [1024, 3072], P(('rep', 'shard'))
- new_first_out: float32 [1024, 1024], P(('rep', 'shard'))
- new_first_up: float32 [1024, 4096], P(('rep', 'shard'))
- new_first_down: float32 [4096, 1024], P(('rep', 'shard'))
- new_first_vec: float32 [13, 1024], P(None, ('rep', 'shard'))
- new_second_qkv: float32 [1024, 3072], P(('rep', 'shard'))
- new_second_out: float32 [1024, 1024], P(('rep', 'shard'))
- new_second_up: float32 [1024, 4096], P(('rep', 'shard'))
- new_second_down: float32 [4096, 1024], P(('rep', 'shard'))
- new_second_vec: float32 [13, 1024], P(None, ('rep', 'shard'))
Inputs may be any that keep to these rules, and one draw needn't show every extreme that they name: `segments`: in every row the segment numbers never fall; each of the 4 numbers covers 1 to 224 consecutive positions and one covers exactly 224. `vectors`: rows 0 and 2 lie in 0.5 to 1.5.
All inputs are finite; a program needn't handle non-finite values.
Results may differ from a plain program's by a relative error of at most 0.019.
The roundings to bfloat16 on the way count: a program that leaves them out, or rounds other values in their place, can miss the bound.
Values may be sent and summed in bfloat16 or wider, within the bound.
No kernel may reach another device: no remote copies, remote signals or barrier semaphores. Data moves between devices by JAX's collectives and lax.ppermute only.
A program may use at most 320 MiB of HBM per device.

v0:
```python
import jax
import jax.numpy as jnp
from jax import lax
from jax.sharding import PartitionSpec as P

D = 1024
HEADS = 16
FF = 4096
ROT = 16
STEP = 10
LN_EPS = 1e-05
BETA_ONE = 0.9
BETA_TWO = 0.95
ADAM_EPS = 1e-08
LR_MATRIX = 0.03
LR_VECTOR = 0.2
WEIGHT_DECAY = 0.01
ROPE_BASE = 10000.0
INV_ROOT_TWO = 0.7071067811865476
INV_ROOT_TAU = 0.3989422804014327


def layer_norm(values, gain, shift):
    center = values - jnp.mean(values, axis=-1, keepdims=True)
    inv_std = lax.rsqrt(jnp.mean(center * center, axis=-1, keepdims=True) + LN_EPS)
    normed = center * inv_std
    return (normed * gain + shift, normed, inv_std)


def norm_backward(upstream, normed, inv_std, gain):
    scaled = upstream * gain
    result = inv_std * (
        scaled
        - jnp.mean(scaled, axis=-1, keepdims=True)
        - normed * jnp.mean(scaled * normed, axis=-1, keepdims=True)
    )
    return (result, jnp.sum(upstream * normed, axis=0), jnp.sum(upstream, axis=0))


def rope_tables(positions):
    half_rot = ROT // 2
    freqs = ROPE_BASE ** (-(2.0 * jnp.arange(half_rot).astype(jnp.float32) / ROT))
    angles = positions.astype(jnp.float32)[:, None] * freqs[None, :]
    return (jnp.cos(angles)[:, None, :], jnp.sin(angles)[:, None, :])


def rotate(heads, cosines, sines):
    half_rot = ROT // 2
    lower = heads[..., :half_rot]
    upper = heads[..., half_rot:ROT]
    return jnp.concatenate(
        [lower * cosines - upper * sines, upper * cosines + lower * sines, heads[..., ROT:]],
        axis=-1,
    )


def unrotate(heads, cosines, sines):
    half_rot = ROT // 2
    lower = heads[..., :half_rot]
    upper = heads[..., half_rot:ROT]
    return jnp.concatenate(
        [lower * cosines + upper * sines, upper * cosines - lower * sines, heads[..., ROT:]],
        axis=-1,
    )


def gelu_value(inner):
    return 0.5 * inner * (1.0 + jax.scipy.special.erf(inner * INV_ROOT_TWO))


def gelu_slope(inner):
    return (
        0.5 * (1.0 + jax.scipy.special.erf(inner * INV_ROOT_TWO))
        + inner * jnp.exp(-0.5 * inner * inner) * INV_ROOT_TAU
    )


def adam_update(param, grad, first, second, rate, decay):
    first_new = BETA_ONE * first + (1.0 - BETA_ONE) * grad
    second_new = BETA_TWO * second + (1.0 - BETA_TWO) * grad * grad
    first_hat = first_new / (1.0 - BETA_ONE**STEP)
    second_hat = second_new / (1.0 - BETA_TWO**STEP)
    return (
        param - rate * (first_hat / (jnp.sqrt(second_hat) + ADAM_EPS) + decay * param),
        first_new,
        second_new,
    )


def contract_rows(left, right):
    return lax.dot_general(
        left, right, (((0,), (0,)), ((), ())), preferred_element_type=jnp.float32
    )


def contract_cols(left, right):
    return lax.dot_general(
        left, right, (((1,), (1,)), ((), ())), preferred_element_type=jnp.float32
    )


def shards(
    block_in,
    cotangent,
    segments,
    qkv_weight,
    out_weight,
    up_weight,
    down_weight,
    vectors,
    first_qkv,
    first_out,
    first_up,
    first_down,
    first_vec,
    second_qkv,
    second_out,
    second_up,
    second_down,
    second_vec,
):
    bf16 = jnp.bfloat16
    tok_count = block_in.shape[0]
    n_shard = lax.axis_size("shard")
    seq_len = tok_count * n_shard
    head_dim = D // HEADS
    per_row = FF // D
    own_rows = qkv_weight.shape[0]
    score_scale = head_dim ** (-0.5)
    vec_all = lax.all_gather(vectors, ("rep", "shard"), axis=1, tiled=True)
    gain_one, shift_one, gain_two, shift_two = (vec_all[0], vec_all[1], vec_all[2], vec_all[3])
    qkv_bias = vec_all[4:7].reshape(3 * D)
    out_bias = vec_all[7]
    up_bias = vec_all[8 : 8 + per_row].reshape(FF)
    down_bias = vec_all[8 + per_row]
    ln_one, normed_one, inv_one = layer_norm(block_in, gain_one, shift_one)
    ln_two, normed_two, inv_two = layer_norm(block_in, gain_two, shift_two)
    h_one = ln_one.astype(bf16)
    h_two = ln_two.astype(bf16)
    in_table = jnp.concatenate([qkv_weight.astype(bf16), up_weight.astype(bf16)], axis=1)
    out_table = jnp.concatenate(
        [out_weight.astype(bf16), down_weight.astype(bf16).reshape(own_rows, per_row * D)], axis=1
    )
    in_whole = lax.all_gather(in_table, ("rep", "shard"), axis=0, tiled=True)
    qkv_lin = jnp.dot(h_one, in_whole[:, : 3 * D], preferred_element_type=jnp.float32) + qkv_bias
    up_lin = jnp.dot(h_two, in_whole[:, 3 * D :], preferred_element_type=jnp.float32) + up_bias
    offset = lax.axis_index("shard") * tok_count
    query_pos = offset + jnp.arange(tok_count)
    key_pos = jnp.arange(seq_len)
    cosines, sines = rope_tables(query_pos)
    query16 = rotate(qkv_lin[:, :D].reshape(tok_count, HEADS, head_dim), cosines, sines).astype(
        bf16
    )
    key16 = (
        rotate(qkv_lin[:, D : 2 * D].reshape(tok_count, HEADS, head_dim), cosines, sines)
        .reshape(tok_count, D)
        .astype(bf16)
    )
    value16 = qkv_lin[:, 2 * D :].astype(bf16)
    keys_all, values_all = (
        lax.all_gather(key16, "shard", axis=0, tiled=True),
        lax.all_gather(value16, "shard", axis=0, tiled=True),
    )
    keys3 = keys_all.reshape(seq_len, HEADS, head_dim)
    values3 = values_all.reshape(seq_len, HEADS, head_dim)
    seg_row = segments[0]
    seg_query = lax.dynamic_slice_in_dim(seg_row, offset, tok_count)
    allowed = (seg_query[:, None] == seg_row[None, :]) & (key_pos[None, :] <= query_pos[:, None])
    scores = jnp.where(
        allowed[None],
        jnp.einsum("qhd,khd->hqk", query16, keys3, preferred_element_type=jnp.float32)
        * score_scale,
        -jnp.inf,
    )
    row_max = jnp.max(scores, axis=-1, keepdims=True)
    expo = jnp.exp(scores - row_max)
    row_sum = jnp.sum(expo, axis=-1, keepdims=True)
    log_total = row_max + jnp.log(row_sum)
    probs16 = (expo / row_sum).astype(bf16)
    mixed16 = (
        jnp.einsum("hqk,khd->qhd", probs16, values3, preferred_element_type=jnp.float32)
        .reshape(tok_count, D)
        .astype(bf16)
    )
    act16 = gelu_value(up_lin).astype(bf16)
    act3 = act16.reshape(tok_count, D, per_row)
    out_whole = lax.all_gather(out_table, ("rep", "shard"), axis=0, tiled=True)
    branches = jnp.dot(mixed16, out_whole[:, :D], preferred_element_type=jnp.float32)
    branches = branches + jnp.dot(
        act16, out_whole[:, D:].reshape(FF, D), preferred_element_type=jnp.float32
    )
    block_out = block_in + branches + out_bias + down_bias
    upstream16 = cotangent.astype(bf16)
    piece = lax.all_gather(out_table, ("rep", "shard"), axis=0, tiled=True)
    num_rows = piece.shape[0]
    first_part = contract_cols(upstream16, piece[:, :D])
    second_part = contract_cols(upstream16, piece[:, D:].reshape(num_rows * per_row, D)).reshape(
        tok_count, num_rows, per_row
    )
    back_table = jnp.concatenate([first_part[:, :, None], second_part], axis=2)
    d_mixed = back_table[:, :, 0]
    d_act = back_table[:, :, 1:].reshape(tok_count, FF)
    d_up = d_act * gelu_slope(up_lin)
    d_up16 = d_up.astype(bf16)
    d_mixed16 = d_mixed.astype(bf16).reshape(tok_count, HEADS, head_dim)
    row_delta = jnp.sum(
        d_mixed16.astype(jnp.float32)
        * mixed16.reshape(tok_count, HEADS, head_dim).astype(jnp.float32),
        axis=-1,
    ).T[:, :, None]
    scores_again = jnp.where(
        allowed[None],
        jnp.einsum("qhd,khd->hqk", query16, keys3, preferred_element_type=jnp.float32)
        * score_scale,
        -jnp.inf,
    )
    probs_again = jnp.exp(scores_again - log_total)
    d_probs = jnp.einsum("qhd,khd->hqk", d_mixed16, values3, preferred_element_type=jnp.float32)
    d_scores16 = (probs_again * (d_probs - row_delta) * score_scale).astype(bf16)
    probs_back16 = probs_again.astype(bf16)
    d_query = jnp.einsum("hqk,khd->qhd", d_scores16, keys3, preferred_element_type=jnp.float32)
    d_keys = jnp.einsum(
        "hqk,qhd->khd", d_scores16, query16, preferred_element_type=jnp.float32
    ).reshape(seq_len, D)
    d_values = jnp.einsum(
        "hqk,qhd->khd", probs_back16, d_mixed16, preferred_element_type=jnp.float32
    ).reshape(seq_len, D)
    own_dkeys, own_dvalues = (
        lax.psum_scatter(d_keys, "shard", scatter_dimension=0, tiled=True),
        lax.psum_scatter(d_values, "shard", scatter_dimension=0, tiled=True),
    )
    d_qkv = jnp.concatenate(
        [
            unrotate(d_query, cosines, sines).reshape(tok_count, D),
            unrotate(own_dkeys.reshape(tok_count, HEADS, head_dim), cosines, sines).reshape(
                tok_count, D
            ),
            own_dvalues,
        ],
        axis=1,
    )
    d_qkv16 = d_qkv.astype(bf16)
    piece = lax.all_gather(in_table, ("rep", "shard"), axis=0, tiled=True)
    first_part = contract_cols(d_qkv16, piece[:, : 3 * D])
    second_part = contract_cols(d_up16, piece[:, 3 * D :])
    norm_table = jnp.stack([first_part, second_part], axis=2)
    d_one = norm_table[:, :, 0]
    d_two = norm_table[:, :, 1]
    dx_one, dgain_one, dshift_one = norm_backward(d_one, normed_one, inv_one, gain_one)
    dx_two, dgain_two, dshift_two = norm_backward(d_two, normed_two, inv_two, gain_two)
    grad_input = cotangent + dx_one + dx_two
    cot_sum = jnp.sum(cotangent, axis=0)
    vec_terms = jnp.concatenate(
        [
            dgain_one[None],
            dshift_one[None],
            dgain_two[None],
            dshift_two[None],
            jnp.sum(d_qkv, axis=0).reshape(3, D),
            cot_sum[None],
            jnp.sum(d_up, axis=0).reshape(per_row, D),
            cot_sum[None],
        ],
        axis=0,
    )
    grad_vec = lax.psum_scatter(vec_terms, ("rep", "shard"), scatter_dimension=1, tiled=True)
    one_cols = h_one[:, :, None]
    two_cols = h_two[:, :, None]
    mixed_cols = mixed16[:, :, None]
    term_qkv = contract_rows(one_cols.reshape(tok_count, D), d_qkv16)
    term_up = contract_rows(two_cols.reshape(tok_count, D), d_up16)
    term_out = contract_rows(mixed_cols.reshape(tok_count, D), upstream16)
    term_down = contract_rows(act3.reshape(tok_count, D * per_row), upstream16)
    grad_table = lax.psum_scatter(
        jnp.concatenate([term_qkv, term_up, term_out, term_down.reshape(D, per_row * D)], axis=1),
        ("rep", "shard"),
        scatter_dimension=0,
        tiled=True,
    )
    grad_qkv = grad_table[:, : 3 * D]
    grad_up = grad_table[:, 3 * D : 3 * D + FF]
    grad_out = grad_table[:, 3 * D + FF : 4 * D + FF]
    grad_down = grad_table[:, 4 * D + FF :].reshape(own_rows * per_row, D)
    new_qkv, new_first_qkv, new_second_qkv = adam_update(
        qkv_weight, grad_qkv, first_qkv, second_qkv, LR_MATRIX, WEIGHT_DECAY
    )
    new_out, new_first_out, new_second_out = adam_update(
        out_weight, grad_out, first_out, second_out, LR_MATRIX, WEIGHT_DECAY
    )
    new_up, new_first_up, new_second_up = adam_update(
        up_weight, grad_up, first_up, second_up, LR_MATRIX, WEIGHT_DECAY
    )
    new_down, new_first_down, new_second_down = adam_update(
        down_weight, grad_down, first_down, second_down, LR_MATRIX, WEIGHT_DECAY
    )
    new_vec, new_first_vec, new_second_vec = adam_update(
        vectors, grad_vec, first_vec, second_vec, LR_VECTOR, 0.0
    )
    return (
        block_out,
        grad_input,
        grad_qkv,
        grad_out,
        grad_up,
        grad_down,
        grad_vec,
        new_qkv,
        new_out,
        new_up,
        new_down,
        new_vec,
        new_first_qkv,
        new_first_out,
        new_first_up,
        new_first_down,
        new_first_vec,
        new_second_qkv,
        new_second_out,
        new_second_up,
        new_second_down,
        new_second_vec,
    )


def solution(mesh):
    return jax.shard_map(
        shards,
        mesh=mesh,
        in_specs=(
            P(("rep", "shard"), None),
            P(("rep", "shard"), None),
            P("rep", None),
            P(("rep", "shard"), None),
            P(("rep", "shard"), None),
            P(("rep", "shard"), None),
            P(("rep", "shard"), None),
            P(None, ("rep", "shard")),
            P(("rep", "shard"), None),
            P(("rep", "shard"), None),
            P(("rep", "shard"), None),
            P(("rep", "shard"), None),
            P(None, ("rep", "shard")),
            P(("rep", "shard"), None),
            P(("rep", "shard"), None),
            P(("rep", "shard"), None),
            P(("rep", "shard"), None),
            P(None, ("rep", "shard")),
        ),
        out_specs=(
            P(("rep", "shard"), None),
            P(("rep", "shard"), None),
            P(("rep", "shard"), None),
            P(("rep", "shard"), None),
            P(("rep", "shard"), None),
            P(("rep", "shard"), None),
            P(None, ("rep", "shard")),
            P(("rep", "shard"), None),
            P(("rep", "shard"), None),
            P(("rep", "shard"), None),
            P(("rep", "shard"), None),
            P(None, ("rep", "shard")),
            P(("rep", "shard"), None),
            P(("rep", "shard"), None),
            P(("rep", "shard"), None),
            P(("rep", "shard"), None),
            P(None, ("rep", "shard")),
            P(("rep", "shard"), None),
            P(("rep", "shard"), None),
            P(("rep", "shard"), None),
            P(("rep", "shard"), None),
            P(None, ("rep", "shard")),
        ),
        check_vma=False,
    )
```

profile of v0, /device:TPU:0, one launch (start us, length us, event | category | flops | bytes accessed | tf_op | source)
XLA Modules:
  0.0 970.5 jit_solution(3823819101333165597)
XLA Ops:
  13.3 74.3 %all-gather = f32[32,32,13]{1,2,0:T(8,128)S(1)} all-gather(f32[1,32,13]{1,2,0:T(8,128)S(1)} %bitcast.115), channel_id=1, replica_groups=mesh['rep'=8,'shard'=4] {'rep','shard'}, dimensions={0}, use_global_device_ids=true | all-gather | bytes 54912 | tf_op jit(solution)/shard_map/all_gather | solution.py:130
  88.3 33.2 %all-gather.6.cloned.1.call-done = bf16[1024,7168]{1,0:T(8,128)(2,1)} async-done(((bf16[32,7168]{1,0:T(8,128)(2,1)}), bf16[1024,7168]{1,0:T(8,128)(2,1)}) %all-gather.6.cloned.1.call-update) | async-done | bytes 14680080 | tf_op jit(solution)/shard_map/all_gather | solution.py:144
  121.5 3.8 fusion.14
  129.9 80.1 %all-gather.12.cloned.1.call-done = bf16[1024,5120]{1,0:T(8,128)(2,1)} async-done(((bf16[32,5120]{1,0:T(8,128)(2,1)}), bf16[1024,5120]{1,0:T(8,128)(2,1)}) %all-gather.12.cloned.1.call-update) | async-done | bytes 10485776 | tf_op jit(solution)/shard_map/all_gather | solution.py:187
  210.0 2.3 fusion.45
  212.4 28.5 %all-gather.10.cloned.1.call-done = bf16[512,1024]{0,1:T(8,128)(2,1)} async-done(((bf16[128,1024]{0,1:T(8,128)(2,1)}), bf16[512,1024]{0,1:T(8,128)(2,1)}) %all-gather.10.cloned.1.call-update) | async-done | bytes 1048592 | tf_op jit(solution)/shard_map/all_gather | solution.py:161
  240.9 2.1 fusion.17
  243.0 1.9 copy-done.1
  246.2 23.0 %all-gather.8.cloned.1.call-done = bf16[512,1024]{1,0:T(8,128)(2,1)} async-done(((bf16[128,1024]{1,0:T(8,128)(2,1)}), bf16[512,1024]{1,0:T(8,128)(2,1)}) %all-gather.8.cloned.1.call-update) | async-done | bytes 1048592 | tf_op jit(solution)/shard_map/all_gather | solution.py:162
  270.7 4.5 multiply_reduce_fusion.4
  280.1 4.7 fusion.22
  285.1 8.0 slice.149
  293.0 14.0 %reshape.257 = bf16[4096,1024]{1,0:T(8,128)(2,1)} reshape(bf16[1024,4096]{1,0:T(8,128)(2,1)} %slice.149) | data formatting | bytes 16777216 | tf_op jit(solution)/shard_map/reshape | solution.py:190
  307.0 4.9 fusion.9
  312.9 4.2 fusion.82
  317.1 8.1 fusion.72
  325.2 20.3 %reshape.264 = f32[1024,4096]{1,0:T(8,128)} reshape(f32[4096,1024]{1,0:T(8,128)} %fusion.72) | data formatting | bytes 33554432 | tf_op jit(solution)/shard_map/reshape | solution.py:275
  345.5 9.7 fusion.53
  356.7 2.6 fusion.83
  361.3 1.9 pad_maximum_fusion.2
  363.2 5.9 reduce-scatter.9.cloned.1.call-done
  370.8 5.4 fusion.4
  376.2 7.5 multiply_reduce_fusion
  384.8 7.7 fusion.61
  392.5 34.0 %pad_maximum_fusion = f32[1024,12288]{1,0:T(8,128)} fusion(f32[1024,4096]{1,0:T(8,128)} %reshape.264, f32[1024,1024]{1,0:T(8,128)} %fusion.83, f32[1024,4096]{1,0:T(8,128)} %fusion.53, f32[1024,3072]{1,0:T(8,128)} %fusion.61), kind=kLoop, calls=%fused_computation | loop fusion | flops 37748736 | bytes 100663296 | tf_op jit(solution)/shard_map/concatenate | solution.py:275
  426.5 4.8 fusion.73
  431.4 3.0 fusion.42
  435.6 83.1 %reduce-scatter.13.cloned.1.call-done = f32[32,13]{1,0:T(8,128)} async-done(((f32[1024,13]{1,0:T(8,128)}), f32[32,13]{1,0:T(8,128)}) %reduce-scatter.13.cloned.1.call-update) | async-done | bytes 1680
  520.1 433.9 %reduce-scatter.11.cloned.1.call-done = f32[32,12288]{1,0:T(8,128)} async-done(((f32[1024,12288]{1,0:T(8,128)}), f32[32,12288]{1,0:T(8,128)}) %reduce-scatter.11.cloned.1.call-update) | async-done | bytes 1572880 | tf_op jit(solution)/shard_map/reduce_scatter | solution.py:274
  954.0 2.6 multiply_subtract_fusion.1
  956.8 2.9 multiply_subtract_fusion
  961.5 2.2 multiply_subtract_fusion.2
  (136 shorter events, 30.8 us)
Async XLA Ops:
  7.2 6.1 copy-start.27
  7.2 80.6 %copy-start.3 = (f32[128,1024]{1,0:T(8,128)S(1)}, f32[128,1024]{1,0:T(8,128)}, u32[]{:S(2)}) copy-start(f32[128,1024]{1,0:T(8,128)} %param.18) | copy-start | bytes 1572868
  7.2 114.3 %all-gather.6.cloned.1.call-start = ((), (), s32[]{:S(2)}) async-start(), calls=%async_computation.4 | async-start | bytes 15138816 | tf_op jit(solution)/shard_map/all_gather | solution.py:144
  10.2 199.8 %all-gather.12.cloned.1.call-start = ((), (), s32[]{:S(2)}) async-start(), calls=%async_computation.7 | async-start | bytes 10813440 | tf_op jit(solution)/shard_map/all_gather | solution.py:187
  13.2 227.7 %all-gather.10.cloned.1.call-start = ((), (), s32[]{:S(2)}) async-start(), calls=%async_computation.6 | async-start | bytes 1310720 | tf_op jit(solution)/shard_map/all_gather | solution.py:161
  125.4 4.5 copy-start.10
  127.8 141.4 %all-gather.8.cloned.1.call-start = ((), (), s32[]{:S(2)}) async-start(), calls=%async_computation.5 | async-start | bytes 1310720 | tf_op jit(solution)/shard_map/all_gather | solution.py:162
  129.7 229.7 %reduce-scatter.7.cloned.1.call-start = ((), (), s32[]{:S(2)}) async-start(), calls=%async_computation.8 | async-start | bytes 2621440 | tf_op jit(solution)/shard_map/reduce_scatter | solution.py:229
  270.7 4.5 copy-start.2
  280.1 89.0 %reduce-scatter.9.cloned.1.call-start = ((), (), s32[]{:S(2)}) async-start(), calls=%async_computation.9 | async-start | bytes 2621440 | tf_op jit(solution)/shard_map/reduce_scatter | solution.py:230
  284.8 233.8 %reduce-scatter.13.cloned.1.call-start = ((), (), s32[]{:S(2)}) async-start(), calls=%async_computation.11 | async-start | bytes 540672
  307.0 5.8 copy-start
  345.4 9.7 copy-start.5
  345.4 9.7 copy-start.6
  370.7 5.4 copy-start.14
  376.2 7.5 copy-start.19
  384.8 569.3 %reduce-scatter.11.cloned.1.call-start = ((), (), s32[]{:S(2)}) async-start(), calls=%async_computation.10 | async-start | bytes 51904512 | tf_op jit(solution)/shard_map/reduce_scatter | solution.py:274
  426.5 4.9 copy-start.16
  431.3 88.1 %copy-start.29 = (f32[13,32]{1,0:T(8,128)S(1)}, f32[13,32]{1,0:T(8,128)}, u32[]{:S(2)}) copy-start(f32[13,32]{1,0:T(8,128)} %param.30) | copy-start | bytes 4996
  431.3 88.1 %copy-start.30 = (f32[13,32]{1,0:T(8,128)S(1)}, f32[13,32]{1,0:T(8,128)}, u32[]{:S(2)}) copy-start(f32[13,32]{1,0:T(8,128)} %param.35) | copy-start | bytes 4996
  431.3 522.7 %copy-start.7 = (f32[32,4096]{1,0:T(8,128)S(1)}, f32[32,4096]{1,0:T(8,128)}, u32[]{:S(2)}) copy-start(f32[32,4096]{1,0:T(8,128)} %param.23) | copy-start | bytes 1572868
  431.4 522.7 %copy-start.17 = (f32[32,4096]{1,0:T(8,128)S(1)}, f32[32,4096]{1,0:T(8,128)}, u32[]{:S(2)}) copy-start(f32[32,4096]{1,0:T(8,128)} %param.28) | copy-start | bytes 1572868
  431.4 522.7 %copy-start.18 = (f32[32,4096]{1,0:T(8,128)S(1)}, f32[32,4096]{1,0:T(8,128)}, u32[]{:S(2)}) copy-start(f32[32,4096]{1,0:T(8,128)} %param.33) | copy-start | bytes 1572868
  434.5 522.3 %copy-start.8 = (f32[128,1024]{1,0:T(8,128)S(1)}, f32[128,1024]{1,0:T(8,128)}, u32[]{:S(2)}) copy-start(f32[128,1024]{1,0:T(8,128)} %param.24) | copy-start | bytes 1572868
  519.5 440.3 %copy-start.28 = (f32[13,32]{1,0:T(8,128)}, f32[13,32]{1,0:T(8,128)S(1)}, u32[]{:S(2)}) copy-start(f32[13,32]{1,0:T(8,128)S(1)} %copy.63) | copy-start | bytes 4996
  520.1 439.6 %copy-start.22 = (f32[32,1024]{1,0:T(8,128)S(1)}, f32[32,1024]{1,0:T(8,128)}, u32[]{:S(2)}) copy-start(f32[32,1024]{1,0:T(8,128)} %param.22) | copy-start | bytes 393220
  520.1 439.6 %copy-start.25 = (f32[32,1024]{1,0:T(8,128)S(1)}, f32[32,1024]{1,0:T(8,128)}, u32[]{:S(2)}) copy-start(f32[32,1024]{1,0:T(8,128)} %param.27) | copy-start | bytes 393220
  520.1 439.6 %copy-start.26 = (f32[32,1024]{1,0:T(8,128)S(1)}, f32[32,1024]{1,0:T(8,128)}, u32[]{:S(2)}) copy-start(f32[32,1024]{1,0:T(8,128)} %param.32) | copy-start | bytes 393220
  956.6 4.8 copy-start.12
  956.6 4.8 copy-start.23
  956.7 4.8 copy-start.24
  956.8 6.9 copy-start.9
  (8 other events, 18.0 us)
Sparse Core Ops, SparseCore 0:
  11.5 110.0 all-gather.5
  124.9 85.0 all-gather.11
  212.2 28.6 all-gather.9
  242.9 26.2 all-gather.7
  280.2 43.3 reduce-scatter.6
  325.8 43.1 reduce-scatter.8
  384.9 133.7 reduce-scatter.12
  526.2 427.7 reduce-scatter.10
where the time goes:
time: 972 us; the launch traced here: 971 us
  waiting for transfers between devices  688 us (71%)
  matrix products  79.6 us (8%)
  blocking collectives  74.3 us (8%)
  other arithmetic  58 us (6%)
  local copies, waits for them, and re-layouts  55.7 us (6%)
  between operations  14.7 us (2%)
    reduce_scatter x1, waiting for transfers between devices, shards(): lax.psum_scatter(jnp.concatenate([term_qkv, term_up, term_out, term_down....  434 us
    unnamed x9, waiting for transfers between devices  83.2 us
    all_gather x1, waiting for transfers between devices, shards(): out_whole = lax.all_gather(out_table, ('rep', 'shard'), axis=0, tiled=True)  80.1 us
    all_gather x1, blocking collectives, shards(): vec_all = lax.all_gather(vectors, ('rep', 'shard'), axis=1, tiled=True)  74.3 us
    concatenate x1, other arithmetic, shards(): jnp.concatenate([term_qkv, term_up, term_out, term_down.reshape(D, per_ro...  34 us
    all_gather x1, waiting for transfers between devices, shards(): in_whole = lax.all_gather(in_table, ('rep', 'shard'), axis=0, tiled=True)  33.2 us
    all_gather x1, waiting for transfers between devices, shards(): lax.all_gather(key16, 'shard', axis=0, tiled=True)  28.5 us
    dot_general x4, matrix products, contract_rows(): lax.dot_general(left, right, (((0,), (0,)), ((), ())), preferred_element_...  28.1 us
  transfers between devices with their start and end apart: 8, of which 7 were waited for; matrix products, arithmetic and copies ran while one was open for 15% of the time, Pallas kernels for 0%

commit v1 on v0

--- a/solution.py
+++ b/solution.py
@@ -18,6 +18,27 @@
 ROPE_BASE = 10000.0
 INV_ROOT_TWO = 0.7071067811865476
 INV_ROOT_TAU = 0.3989422804014327
+
+
+def gather_around(x, axis, dim):
+    devices, index, rows = (lax.axis_size(axis), lax.axis_index(axis), x.shape[dim])
+    ahead = [(i, (i + 1) % devices) for i in range(devices)]
+    downward = [(i, (i - 1) % devices) for i in range(devices)]
+    out = jnp.zeros((*x.shape[:dim], devices * rows, *x.shape[dim + 1 :]), x.dtype)
+    out = lax.dynamic_update_slice_in_dim(out, x, index * rows, axis=dim)
+    from_left = from_right = x
+    middle = devices // 2
+    for step in range(1, middle + 1):
+        from_left = lax.ppermute(from_left, axis, ahead)
+        out = lax.dynamic_update_slice_in_dim(
+            out, from_left, (index - step) % devices * rows, axis=dim
+        )
+        if step < devices - middle:
+            from_right = lax.ppermute(from_right, axis, downward)
+            out = lax.dynamic_update_slice_in_dim(
+                out, from_right, (index + step) % devices * rows, axis=dim
+            )
+    return out
 
 
 def layer_norm(values, gain, shift):
@@ -159,7 +180,7 @@
     value16 = qkv_lin[:, 2 * D :].astype(bf16)
     keys_all, values_all = (
         lax.all_gather(key16, "shard", axis=0, tiled=True),
-        lax.all_gather(value16, "shard", axis=0, tiled=True),
+        gather_around(value16, "shard", 0),
     )
     keys3 = keys_all.reshape(seq_len, HEADS, head_dim)
     values3 = values_all.reshape(seq_len, HEADS, head_dim)

time: 972 us -> 948 us (0.975)
  waiting for transfers between devices: 688 us -> 659 us
    all_gather x1 -> x0, waiting for transfers between devices: 23 us -> none  [shards(): lax.all_gather(value16, 'shard', axis=0, tiled=True)]
    all_gather x1, waiting for transfers between devices: 28.5 us -> 16.1 us  [shards(): lax.all_gather(key16, 'shard', axis=0, tiled=True)]
    unnamed x9 -> x8, waiting for transfers between devices: 83.2 us -> 82.7 us
  transfers between devices with their start and end apart: 8 -> 10, of which waited for: 7 -> 7; matrix products, arithmetic and copies ran while one was open for 15% -> 16% of each run, Pallas kernels for 0% -> 0%
where the time goes in v1:
time: 948 us; the launch traced here: 947 us
  waiting for transfers between devices  659 us (70%)
  matrix products  77.5 us (8%)
  blocking collectives  74.3 us (8%)
  other arithmetic  58.6 us (6%)
  local copies, waits for them, and re-layouts  56.5 us (6%)
  between operations  15 us (2%)
    reduce_scatter x1, waiting for transfers between devices, shards(): lax.psum_scatter(jnp.concatenate([term_qkv, term_up, term_out, term_down....  434 us
    unnamed x8, waiting for transfers between devices  82.7 us
    all_gather x1, waiting for transfers between devices, shards(): out_whole = lax.all_gather(out_table, ('rep', 'shard'), axis=0, tiled=True)  81.8 us
    all_gather x1, blocking collectives, shards(): vec_all = lax.all_gather(vectors, ('rep', 'shard'), axis=1, tiled=True)  74.3 us
    concatenate x1, other arithmetic, shards(): jnp.concatenate([term_qkv, term_up, term_out, term_down.reshape(D, per_ro...  34.1 us
    all_gather x1, waiting for transfers between devices, shards(): in_whole = lax.all_gather(in_table, ('rep', 'shard'), axis=0, tiled=True)  32.6 us
    dot_general x4, matrix products, contract_rows(): lax.dot_general(left, right, (((0,), (0,)), ((), ())), preferred_element_...  28.1 us
    reshape x1, local copies, waits for them, and re-layouts, shards(): term_down.reshape(D, per_row * D)  20.4 us
  transfers between devices with their start and end apart: 10, of which 7 were waited for; matrix products, arithmetic and copies ran while one was open for 16% of the time, Pallas kernels for 0%

profile of v1, /device:TPU:0, one launch (start us, length us, event | category | flops | bytes accessed | tf_op | source)
XLA Modules:
  0.0 946.9 jit_solution(17721631060173392767)
XLA Ops:
  13.3 74.3 %all-gather = f32[32,32,13]{1,2,0:T(8,128)S(1)} all-gather(f32[1,32,13]{1,2,0:T(8,128)S(1)} %bitcast.115), channel_id=1, replica_groups=mesh['rep'=8,'shard'=4] {'rep','shard'}, dimensions={0}, use_global_device_ids=true | all-gather | bytes 54912 | tf_op jit(solution)/shard_map/all_gather | solution.py:151
  88.9 32.6 %all-gather.5.cloned.1.call-done = bf16[1024,7168]{1,0:T(8,128)(2,1)} async-done(((bf16[32,7168]{1,0:T(8,128)(2,1)}), bf16[1024,7168]{1,0:T(8,128)(2,1)}) %all-gather.5.cloned.1.call-update) | async-done | bytes 14680080 | tf_op jit(solution)/shard_map/all_gather | solution.py:165
  121.5 3.8 fusion.14
  130.5 3.2 collective-permute-start.1
  133.7 81.8 %all-gather.9.cloned.1.call-done = bf16[1024,5120]{1,0:T(8,128)(2,1)} async-done(((bf16[32,5120]{1,0:T(8,128)(2,1)}), bf16[1024,5120]{1,0:T(8,128)(2,1)}) %all-gather.9.cloned.1.call-update) | async-done | bytes 10485776 | tf_op jit(solution)/shard_map/all_gather | solution.py:208
  215.5 2.3 fusion.45
  222.5 6.1 collective-permute-done.2
  229.5 16.1 %all-gather.7.cloned.1.call-done = bf16[512,1024]{0,1:T(8,128)(2,1)} async-done(((bf16[128,1024]{0,1:T(8,128)(2,1)}), bf16[512,1024]{0,1:T(8,128)(2,1)}) %all-gather.7.cloned.1.call-update) | async-done | bytes 1048592 | tf_op jit(solution)/shard_map/all_gather | solution.py:182
  245.6 2.2 fusion.17
  249.0 2.3 multiply_reduce_fusion.4
  256.2 4.7 fusion.22
  261.2 8.1 slice.149
  269.4 14.0 %reshape.257 = bf16[4096,1024]{1,0:T(8,128)(2,1)} reshape(bf16[1024,4096]{1,0:T(8,128)(2,1)} %slice.149) | data formatting | bytes 16777216 | tf_op jit(solution)/shard_map/reshape | solution.py:211
  283.3 4.9 fusion.9
  289.1 4.2 fusion.83
  293.3 8.1 fusion.73
  301.5 20.4 %reshape.264 = f32[1024,4096]{1,0:T(8,128)} reshape(f32[4096,1024]{1,0:T(8,128)} %fusion.73) | data formatting | bytes 33554432 | tf_op jit(solution)/shard_map/reshape | solution.py:296
  321.8 9.7 %fusion.53 = f32[1024,4096]{1,0:T(8,128)} fusion(bf16[128,4096]{1,0:T(8,128)(2,1)} %get-tuple-element.82, f32[1024]{0:T(1024)S(1)} %bitcast.110, f32[1024]{0:T(1024)S(1)} %bitcast.102, f32[128,1024]{1,0:T(8,128)S(1)} %copy-done.2, f32[128]{0:T(128)S(1)} %copy-done.41, f32[128]{0:T(128)S(1)} %copy-done.37), kind=kOutput, calls=%fused_computation.64 | convolution fusion | flops 1074397184 | bytes 18359296 | tf_op jit(solution)/shard_map/dot_general | solution.py:112
  333.1 2.7 fusion.84
  337.7 1.9 pad_maximum_fusion.2
  339.6 5.9 reduce-scatter.9.cloned.1.call-done
  347.3 5.4 fusion.4
  352.7 7.5 multiply_reduce_fusion
  361.3 7.6 fusion.61
  369.0 34.1 %pad_maximum_fusion = f32[1024,12288]{1,0:T(8,128)} fusion(f32[1024,4096]{1,0:T(8,128)} %reshape.264, f32[1024,1024]{1,0:T(8,128)} %fusion.84, f32[1024,4096]{1,0:T(8,128)} %fusion.53, f32[1024,3072]{1,0:T(8,128)} %fusion.61), kind=kLoop, calls=%fused_computation | loop fusion | flops 37748736 | bytes 100663296 | tf_op jit(solution)/shard_map/concatenate | solution.py:296
  403.1 4.8 fusion.74
  408.0 3.0 fusion.42
  412.2 82.6 %reduce-scatter.13.cloned.1.call-done = f32[32,13]{1,0:T(8,128)} async-done(((f32[1024,13]{1,0:T(8,128)}), f32[32,13]{1,0:T(8,128)}) %reduce-scatter.13.cloned.1.call-update) | async-done | bytes 1680
  496.2 434.1 %reduce-scatter.11.cloned.1.call-done = f32[32,12288]{1,0:T(8,128)} async-done(((f32[1024,12288]{1,0:T(8,128)}), f32[32,12288]{1,0:T(8,128)}) %reduce-scatter.11.cloned.1.call-update) | async-done | bytes 1572880 | tf_op jit(solution)/shard_map/reduce_scatter | solution.py:295
  930.4 2.6 multiply_subtract_fusion.1
  933.2 2.9 multiply_subtract_fusion
  937.8 2.2 multiply_subtract_fusion.2
  (173 shorter events, 36.0 us)
Async XLA Ops:
  7.2 80.6 %copy-start.2 = (f32[128,1024]{1,0:T(8,128)S(1)}, f32[128,1024]{1,0:T(8,128)}, u32[]{:S(2)}) copy-start(f32[128,1024]{1,0:T(8,128)} %param.18) | copy-start | bytes 1572868
  7.2 114.3 %all-gather.5.cloned.1.call-start = ((), (), s32[]{:S(2)}) async-start(), calls=%async_computation.4 | async-start | bytes 15138816 | tf_op jit(solution)/shard_map/all_gather | solution.py:165
  10.2 205.3 %all-gather.9.cloned.1.call-start = ((), (), s32[]{:S(2)}) async-start(), calls=%async_computation.6 | async-start | bytes 10813440 | tf_op jit(solution)/shard_map/all_gather | solution.py:208
  13.2 232.3 %all-gather.7.cloned.1.call-start = ((), (), s32[]{:S(2)}) async-start(), calls=%async_computation.5 | async-start | bytes 1310720 | tf_op jit(solution)/shard_map/all_gather | solution.py:182
  87.9 37.4 %copy-start.36 = (f32[128]{0:T(128)}, f32[128]{0:T(128)S(1)}, u32[]{:S(2)}) copy-start(f32[128]{0:T(128)S(1)} %broadcast_multiply_fusion.4) | copy-start | bytes 1540
  88.2 37.2 %copy-start.40 = (f32[128]{0:T(128)}, f32[128]{0:T(128)S(1)}, u32[]{:S(2)}) copy-start(f32[128]{0:T(128)S(1)} %add_rsqrt_fusion) | copy-start | bytes 1540
  88.3 38.7 %copy-start.28 = (f32[128,8]{0,1:T(8,128)}, f32[128,8]{0,1:T(8,128)S(1)}, u32[]{:S(2)}) copy-start(f32[128,8]{0,1:T(8,128)S(1)} %get-tuple-element.74) | copy-start | bytes 12292
  88.3 38.7 %copy-start.30 = (f32[128,8]{0,1:T(8,128)}, f32[128,8]{0,1:T(8,128)S(1)}, u32[]{:S(2)}) copy-start(f32[128,8]{0,1:T(8,128)S(1)} %get-tuple-element.75) | copy-start | bytes 12292
  127.8 207.9 %reduce-scatter.7.cloned.1.call-start = ((), (), s32[]{:S(2)}) async-start(), calls=%async_computation.7 | async-start | bytes 2621440 | tf_op jit(solution)/shard_map/reduce_scatter | solution.py:250
  129.8 88.2 %collective-permute-start = (bf16[128,1024]{1,0:T(8,128)(2,1)S(1)}, bf16[128,1024]{1,0:T(8,128)(2,1)S(1)}, u32[]{:S(2)}, u32[]{:S(2)}) collective-permute-start(bf16[128,1024]{1,0:T(8,128)(2,1)S(1)} %slice.208), channel_id=1, source_target_pairs={{0,1},{1,2},{2,3},{3,0},{4,5},{5,6},{6,7},{7,4},{8,9},{9,10},{10,1... | collective-permute-start | bytes 786440 | tf_op jit(solution)/shard_map/ppermute | solution.py:32
  130.5 90.3 %collective-permute-start.1 = (bf16[128,1024]{1,0:T(8,128)(2,1)S(1)}, bf16[128,1024]{1,0:T(8,128)(2,1)S(1)}, u32[]{:S(2)}, u32[]{:S(2)}) collective-permute-start(bf16[128,1024]{1,0:T(8,128)(2,1)S(1)} %slice.208), channel_id=1, source_target_pairs={{0,3},{1,0},{2,1},{3,2},{4,7},{5,4},{6,5},{7,6},{8,11},{9,8},{10,9... | collective-permute-start | bytes 786440 | tf_op jit(solution)/shard_map/ppermute | solution.py:37
  218.0 10.5 %collective-permute-start.2 = (bf16[128,1024]{1,0:T(8,128)(2,1)S(1)}, bf16[128,1024]{1,0:T(8,128)(2,1)S(1)}, u32[]{:S(2)}, u32[]{:S(2)}) collective-permute-start(bf16[128,1024]{1,0:T(8,128)(2,1)S(1)} %collective-permute-done), channel_id=1, source_target_pairs={{0,1},{1,2},{2,3},{3,0},{4,5},{5,6},{6,7},{7,4},{8,9},{9,10},{10,1... | collective-permute-start | bytes 786440 | tf_op jit(solution)/shard_map/ppermute | solution.py:32
  256.2 89.4 %reduce-scatter.9.cloned.1.call-start = ((), (), s32[]{:S(2)}) async-start(), calls=%async_computation.8 | async-start | bytes 2621440 | tf_op jit(solution)/shard_map/reduce_scatter | solution.py:251
  261.0 233.8 %reduce-scatter.13.cloned.1.call-start = ((), (), s32[]{:S(2)}) async-start(), calls=%async_computation.10 | async-start | bytes 540672
  269.4 14.0 %copy-start.37 = (f32[128]{0:T(128)S(1)}, f32[128]{0:T(128)}, u32[]{:S(2)}) copy-start(f32[128]{0:T(128)} %copy-done.36) | copy-start | bytes 1540
  269.4 14.0 %copy-start.41 = (f32[128]{0:T(128)S(1)}, f32[128]{0:T(128)}, u32[]{:S(2)}) copy-start(f32[128]{0:T(128)} %copy-done.40) | copy-start | bytes 1540
  321.8 9.7 %copy-start.4 = (bf16[16,128,512]{2,1,0:T(8,128)(2,1)S(1)}, bf16[16,128,512]{2,1,0:T(8,128)(2,1)}, u32[]{:S(2)}) copy-start(bf16[16,128,512]{2,1,0:T(8,128)(2,1)} %copy-done.3) | copy-start | bytes 6291460
  321.8 9.7 %copy-start.5 = (bf16[512,1024]{0,1:T(8,128)(2,1)S(1)}, bf16[512,1024]{0,1:T(8,128)(2,1)}, u32[]{:S(2)}) copy-start(bf16[512,1024]{0,1:T(8,128)(2,1)} %all-gather.7.cloned.1.call-done) | copy-start | bytes 3145732
  352.7 7.5 copy-start.20
  352.7 7.5 copy-start.32
  361.3 569.1 %reduce-scatter.11.cloned.1.call-start = ((), (), s32[]{:S(2)}) async-start(), calls=%async_computation.9 | async-start | bytes 51904512 | tf_op jit(solution)/shard_map/reduce_scatter | solution.py:295
  407.9 87.7 %copy-start.34 = (f32[13,32]{1,0:T(8,128)S(1)}, f32[13,32]{1,0:T(8,128)}, u32[]{:S(2)}) copy-start(f32[13,32]{1,0:T(8,128)} %param.25) | copy-start | bytes 4996
  407.9 87.7 %copy-start.42 = (f32[13,32]{1,0:T(8,128)S(1)}, f32[13,32]{1,0:T(8,128)}, u32[]{:S(2)}) copy-start(f32[13,32]{1,0:T(8,128)} %param.30) | copy-start | bytes 4996
  407.9 87.7 %copy-start.43 = (f32[13,32]{1,0:T(8,128)S(1)}, f32[13,32]{1,0:T(8,128)}, u32[]{:S(2)}) copy-start(f32[13,32]{1,0:T(8,128)} %param.35) | copy-start | bytes 4996
  407.9 522.4 %copy-start.6 = (f32[32,4096]{1,0:T(8,128)S(1)}, f32[32,4096]{1,0:T(8,128)}, u32[]{:S(2)}) copy-start(f32[32,4096]{1,0:T(8,128)} %param.23) | copy-start | bytes 1572868
  407.9 522.4 %copy-start.18 = (f32[32,4096]{1,0:T(8,128)S(1)}, f32[32,4096]{1,0:T(8,128)}, u32[]{:S(2)}) copy-start(f32[32,4096]{1,0:T(8,128)} %param.28) | copy-start | bytes 1572868
  408.0 522.4 %copy-start.19 = (f32[32,4096]{1,0:T(8,128)S(1)}, f32[32,4096]{1,0:T(8,128)}, u32[]{:S(2)}) copy-start(f32[32,4096]{1,0:T(8,128)} %param.33) | copy-start | bytes 1572868
  411.1 522.1 %copy-start.7 = (f32[128,1024]{1,0:T(8,128)S(1)}, f32[128,1024]{1,0:T(8,128)}, u32[]{:S(2)}) copy-start(f32[128,1024]{1,0:T(8,128)} %param.24) | copy-start | bytes 1572868
  495.6 440.5 %copy-start.35 = (f32[13,32]{1,0:T(8,128)}, f32[13,32]{1,0:T(8,128)S(1)}, u32[]{:S(2)}) copy-start(f32[13,32]{1,0:T(8,128)S(1)} %copy.71) | copy-start | bytes 4996
  496.2 439.8 %copy-start.23 = (f32[32,1024]{1,0:T(8,128)S(1)}, f32[32,1024]{1,0:T(8,128)}, u32[]{:S(2)}) copy-start(f32[32,1024]{1,0:T(8,128)} %param.22) | copy-start | bytes 393220
  496.2 439.8 %copy-start.26 = (f32[32,1024]{1,0:T(8,128)S(1)}, f32[32,1024]{1,0:T(8,128)}, u32[]{:S(2)}) copy-start(f32[32,1024]{1,0:T(8,128)} %param.27) | copy-start | bytes 393220
  496.2 439.8 %copy-start.27 = (f32[32,1024]{1,0:T(8,128)S(1)}, f32[32,1024]{1,0:T(8,128)}, u32[]{:S(2)}) copy-start(f32[32,1024]{1,0:T(8,128)} %param.32) | copy-start | bytes 393220
  (23 other events, 91.0 us)
Sparse Core Ops, SparseCore 0:
  11.5 110.0 all-gather.4
  124.9 90.5 all-gather.8
  217.7 27.8 all-gather.6
  256.3 43.7 reduce-scatter.6
  302.3 43.1 reduce-scatter.8
  361.4 133.3 reduce-scatter.12
  502.3 427.9 reduce-scatter.10
